TPU v7x, 32 devices: a whole 2x2x4 slice. The times are simulated.
32 devices in a mesh: fsdp: 8 (over y, x, core), group: 4 (over z).
Axes of the slice: x: 2, y: 2, z: 4, core: 2. Of those that a mesh axis runs over, the one named last changes fastest.
Arguments:
- gradient: bfloat16 [4, 512, 4096], P('group', 'fsdp'), may hold values from -4000 to 4000
- first_moment: bfloat16 [4, 4096, 512], P('group', 'fsdp'), may hold values from -3 to 3
- second_moment: bfloat16 [4, 4096, 512], P('group', 'fsdp'), may hold values from 0.29882812 to 3
- basis_store: bfloat16 [4, 4608, 256], P('group', 'fsdp'), may hold values from -1 to 2
- step_number: int32 [1], replicated, may hold values from 1 to 99999
- matrix_ids: int32 [4], P('group'), may hold values from 0 to 3, each once
Outputs:
- update: bfloat16 [4, 512, 4096], P('group', 'fsdp')
- new_first: bfloat16 [4, 4096, 512], P('group', 'fsdp')
- new_second: bfloat16 [4, 4096, 512], P('group', 'fsdp')
Inputs may be any that keep to these rules, and one draw needn't show every extreme that they name: `matrix_ids`: each matrix index once.
All inputs are finite; a program needn't handle non-finite values.
Results may differ from a plain program's by a relative error of at most 0.0004.
Values may be sent and summed in bfloat16 or wider, within the bound.
A program may use at most 64 MiB of HBM per device.

v0:
```python
import math
import jax
import jax.numpy as jnp
from jax import lax
from jax.sharding import PartitionSpec as P

BLOCK = 256
BETA_ONE = 0.95
BETA_TWO = 0.95
ADAM_EPS = 1e-08
HIGHEST = lax.Precision.HIGHEST


def clip_of(local_squares, entries):
    total = lax.psum(local_squares, ("fsdp", "group"))
    return jnp.float32(math.sqrt(entries)) / (jnp.sqrt(total) + 1e-06)


def local(gradient, first_moment, second_moment, basis_store, step_number, matrix_ids):
    fsdp_count = lax.axis_size("fsdp")
    group_count = lax.axis_size("group")
    row_count = gradient.shape[1]
    col_count = gradient.shape[2]
    all_rows = row_count * fsdp_count
    col_share = col_count // fsdp_count
    left_blocks = all_rows // BLOCK
    right_blocks = col_count // BLOCK
    entries = all_rows * col_count * group_count
    grad_local = gradient[0].astype(jnp.float32)
    local_squares = jnp.sum(grad_local * grad_local)
    gathered = lax.all_gather(basis_store[0], "fsdp", axis=0, tiled=True)
    owner_rows = basis_store.shape[1]
    owner = (step_number[0] + matrix_ids[0]) % fsdp_count
    ordered_half = jnp.roll(gathered, -owner * owner_rows, axis=0)
    left = ordered_half[:all_rows].astype(jnp.float32).reshape(left_blocks, BLOCK, BLOCK)
    right_half = ordered_half[all_rows:].reshape(right_blocks, BLOCK, BLOCK)
    right = right_half.astype(jnp.float32)
    turned = jnp.einsum(
        "rbj,bjl->rbl",
        gradient[0].reshape(row_count, right_blocks, BLOCK),
        right_half,
        preferred_element_type=jnp.float32,
    )
    turned = clip_of(local_squares, entries) * turned
    outgoing = turned.reshape(row_count, fsdp_count, col_share)
    received = lax.all_to_all(outgoing, "fsdp", split_axis=1, concat_axis=0, tiled=True)
    width = received.shape[2]
    columns = received[:, 0, :].reshape(left_blocks, BLOCK, width)
    rotated = jnp.einsum("bkc,bki->cbi", columns, left, precision=HIGHEST).reshape(width, all_rows)
    count = step_number[0].astype(jnp.float32)
    first_fix = 1.0 - jnp.power(jnp.float32(BETA_ONE), count)
    second_fix = 1.0 - jnp.power(jnp.float32(BETA_TWO), count)
    first_sum = BETA_ONE * first_moment[0].astype(jnp.float32) + (1.0 - BETA_ONE) * rotated
    second_sum = (
        BETA_TWO * second_moment[0].astype(jnp.float32) + (1.0 - BETA_TWO) * rotated * rotated
    )
    direction = first_sum / first_fix / (jnp.sqrt(second_sum / second_fix) + ADAM_EPS)
    backward = jnp.einsum(
        "cbi,bki->cbk", direction.reshape(col_share, left_blocks, BLOCK), left, precision=HIGHEST
    )
    returning = backward.reshape(col_share, fsdp_count, row_count)
    received = lax.all_to_all(returning, "fsdp", split_axis=1, concat_axis=0, tiled=True)
    width = received.shape[2]
    pieces = received[:, 0, :].reshape(right_blocks, BLOCK, width)
    result = jnp.einsum("blr,bjl->rbj", pieces, right, precision=HIGHEST).reshape(width, col_count)
    return (
        result[None].astype(jnp.bfloat16),
        first_sum[None].astype(jnp.bfloat16),
        second_sum[None].astype(jnp.bfloat16),
    )


def solution(mesh):
    in_specs = (
        P("group", "fsdp", None),
        P("group", "fsdp", None),
        P("group", "fsdp", None),
        P("group", "fsdp", None),
        P(),
        P("group"),
    )
    out_specs = (P("group", "fsdp", None), P("group", "fsdp", None), P("group", "fsdp", None))
    return jax.shard_map(local, mesh=mesh, in_specs=in_specs, out_specs=out_specs, check_vma=False)
```

profile of v0, /device:TPU:0, one launch (start us, length us, event | category | flops | bytes accessed | tf_op | source)
XLA Modules:
  0.0 129.9 jit_solution(4664834779437250794)
XLA Ops:
  7.2 0.0 all-gather.3.cloned.1.call-start
  7.2 0.7 all-gather.3.cloned.1.call-update
  7.9 1.9 %multiply_reduce_fusion = f32[]{:T(128)} fusion(bf16[1,64,4096]{2,1,0:T(8,128)(2,1)} %param.6), kind=kLoop, calls=%fused_computation.24 | loop fusion | flops 786431 | bytes 524292 | tf_op jit(solution)/shard_map/reduce_sum | solution.py:30
  9.8 42.2 %psum.7 = f32[]{:T(128)} all-reduce(f32[]{:T(128)} %multiply_reduce_fusion), channel_id=1, replica_groups=mesh['fsdp'=8,'group'=4] {'fsdp','group'}, use_global_device_ids=true, to_apply=%region_1.2 | all-reduce | flops 1 | bytes 8 | tf_op jit(solution)/shard_map/psum | solution.py:15
  54.0 1.1 copy.42
  55.2 0.0 all-gather.3.cloned.1.call-done
  55.3 3.7 %fusion = bf16[4608,256]{1,0:T(8,128)(2,1)S(1)} fusion(s32[]{:T(128)S(6)} %select_n.21, bf16[4608,256]{1,0:T(8,128)(2,1)} %bitcast.46), kind=kLoop, calls=%fused_computation.2 | loop fusion | flops 4718592 | bytes 4718596 | tf_op jit(solution)/shard_map/jit(_roll_dynamic)/concatenate | solution.py:34
  59.0 0.0 copy-start
  59.0 0.1 slice.8
  59.2 0.5 fusion.1
  59.6 0.8 copy-done
  60.4 0.6 copy.30
  61.0 1.3 %reshape.80 = f32[64,8,512]{2,1,0:T(8,128)} reshape(f32[64,16,256]{2,1,0:T(8,128)S(1)} %copy.30) | data formatting | bytes 2097152 | tf_op jit(solution)/shard_map/reshape | solution.py:45
  62.3 2.8 %copy.31 = f32[64,8,512]{2,0,1:T(8,128)} copy(f32[64,8,512]{2,1,0:T(8,128)} %reshape.80) | data formatting | bytes 2097152 | tf_op jit(solution)/shard_map/reshape | solution.py:45
  65.1 3.8 %all-to-all-start = ((f32[64,8,512]{2,0,1:T(8,128)}), f32[64,8,512]{2,0,1:T(8,128)S(1)}, u32[]{:S(2)}, u32[]{:S(2)}) async-start(f32[64,8,512]{2,0,1:T(8,128)} %copy.31), calls=%async_computation | async-start | bytes 2097152 | tf_op jit(solution)/shard_map/all_to_all | solution.py:46
  69.0 1.0 slice.9
  69.9 14.4 %all-to-all-done = f32[64,8,512]{2,0,1:T(8,128)S(1)} async-done(((f32[64,8,512]{2,0,1:T(8,128)}), f32[64,8,512]{2,0,1:T(8,128)S(1)}, u32[]{:S(2)}, u32[]{:S(2)}) %all-to-all-start) | async-done | bytes 1048608 | tf_op jit(solution)/shard_map/all_to_all | solution.py:46
  84.3 1.7 %fusion.23 = f32[2,256,512]{2,1,0:T(8,128)} fusion(bf16[2,256,256]{2,1,0:T(8,128)(2,1)S(1)} %bitcast.49, f32[2,256,512]{2,1,0:T(8,128)S(1)} %bitcast.43), kind=kOutput, calls=%fused_computation.32 | convolution fusion | flops 805306368 | bytes 2359296 | tf_op jit(solution)/shard_map/bkc,bki->cbi/dot_general | solution.py:49
  86.0 2.5 %copy.38 = f32[1,512,512]{2,1,0:T(8,128)} copy(f32[1,512,512]{1,2,0:T(8,128)} %bitcast.44) | data formatting | bytes 2097152 | tf_op jit(solution)/shard_map/reshape | solution.py:49
  88.6 3.0 %fusion.14 = (bf16[1,512,512]{2,1,0:T(8,128)(2,1)}, bf16[1,512,512]{2,1,0:T(8,128)(2,1)}, f32[1,512,512]{2,1,0:T(8,128)}, f32[1,512,512]{2,1,0:T(8,128)S(1)}) fusion(f32[1,512,512]{2,1,0:T(8,128)} %copy.38, bf16[1,512,512]{2,1,0:T(8,128)(2,1)} %param.8, bf16[1,512,512]{2,1,0:T(8,128)(2,1)} %param.7), kind=kLoop, calls=%fused_computation.20 | loop fusion | flops 2621440 | bytes 5242880 | tf_op jit(solution)/shard_map/convert_element_type | solution.py:69
  91.6 2.6 %copy.28 = f32[1,512,512]{1,2,0:T(8,128)} copy(f32[1,512,512]{2,1,0:T(8,128)} %get-tuple-element.5) | data formatting | bytes 2097152 | tf_op jit(solution)/shard_map/mul | solution.py:53
  94.2 1.3 %copy.33 = f32[1,512,512]{1,2,0:T(8,128)} copy(f32[1,512,512]{2,1,0:T(8,128)S(1)} %get-tuple-element.6) | data formatting | bytes 2097152 | tf_op jit(solution)/shard_map/mul | solution.py:55
  95.5 3.1 %fusion.4 = f32[2,256,512]{2,1,0:T(8,128)S(1)} fusion(bf16[2,256,256]{2,1,0:T(8,128)(2,1)S(1)} %bitcast.50, f32[512,2,256]{0,2,1:T(8,128)} %bitcast.51, f32[512,2,256]{0,2,1:T(8,128)} %bitcast.52, f32[2,256,512]{2,1,0:T(8,128)} %fusion.23, f32[]{:T(128)} %bitcast.10), kind=kOutput, calls=%fused_computation.12 | convolution fusion | flops 807403520 | bytes 4456452 | tf_op jit(solution)/shard_map/cbi,bki->cbk/dot_general | solution.py:58
  98.6 17.8 %all_to_all.30 = f32[512,8,64]{0,2,1:T(8,128)S(1)} all-to-all(f32[512,8,64]{0,2,1:T(8,128)S(1)} %bitcast.53), channel_id=1, replica_groups=mesh['fsdp'=8,'group'=4] {'fsdp'}, dimensions={1} | all-to-all | bytes 2097152 | tf_op jit(solution)/shard_map/all_to_all | solution.py:62
  116.4 1.6 %copy.35 = f32[8,512,1,64]{1,0,3,2:T(8,128)} copy(f32[8,512,1,64]{1,3,0,2:T(8,128)S(1)} %bitcast.45) | data formatting | bytes 2097152 | tf_op jit(solution)/shard_map/all_to_all | solution.py:62
  118.0 1.4 %reshape_squeeze.11 = f32[16,256,64]{1,0,2:T(8,128)S(1)} reshape(f32[8,512,1,64]{1,0,3,2:T(8,128)} %copy.35) | data formatting | bytes 2097152 | tf_op jit(solution)/shard_map/reshape;squeeze | solution.py:64
  119.4 2.3 %fusion.2 = bf16[64,16,256]{2,0,1:T(8,128)(2,1)S(1)} fusion(bf16[16,256,256]{2,1,0:T(8,128)(2,1)S(1)} %bitcast.42, f32[16,256,64]{1,0,2:T(8,128)S(1)} %reshape_squeeze.11), kind=kOutput, calls=%fused_computation.10 | convolution fusion | flops 805568512 | bytes 3670016 | tf_op jit(solution)/shard_map/blr,bjl->rbj/dot_general | solution.py:65
  121.7 0.3 copy.37
  122.0 1.0 convert_element_type.55
Async XLA Ops:
  7.2 48.1 %all-gather.3.cloned.1.call-start = ((), (), s32[]{:S(2)}) async-start(), calls=%async_computation.2 | async-start | bytes 2654208 | tf_op jit(solution)/shard_map/all_gather | solution.py:31
  59.0 1.4 %copy-start = (bf16[4608,256]{1,0:T(8,128)(2,1)}, bf16[4608,256]{1,0:T(8,128)(2,1)S(1)}, u32[]{:S(2)}) copy-start(bf16[4608,256]{1,0:T(8,128)(2,1)S(1)} %fusion) | copy-start | bytes 7077892
  65.1 19.2 %all-to-all-start = ((f32[64,8,512]{2,0,1:T(8,128)}), f32[64,8,512]{2,0,1:T(8,128)S(1)}, u32[]{:S(2)}, u32[]{:S(2)}) async-start(f32[64,8,512]{2,0,1:T(8,128)} %copy.31), calls=%async_computation | async-start | bytes 2097152 | tf_op jit(solution)/shard_map/all_to_all | solution.py:46
Sparse Core Ops, SparseCore 0:
  9.9 31.9 all-gather.2
where the time goes:
time: 131 us; the launch traced here: 130 us
  blocking collectives  60 us (46%)
  local copies, waits for them, and re-layouts  18.5 us (14%)
  between operations  16.2 us (12%)
  waiting for transfers between devices  15.1 us (12%)
  other arithmetic  8.67 us (7%)
  matrix products  7.53 us (6%)
  starting transfers between devices  3.82 us (3%)
    psum x1, blocking collectives, clip_of(): total = lax.psum(local_squares, ('fsdp', 'group'))  42.2 us
    all_to_all x1, blocking collectives, local(): lax.all_to_all(returning, 'fsdp', split_axis=1, concat_axis=0, tiled=True)  17.8 us
    all_to_all x1, waiting for transfers between devices, local(): lax.all_to_all(outgoing, 'fsdp', split_axis=1, concat_axis=0, tiled=True)  14.4 us
    reshape x2, local copies, waits for them, and re-layouts, local(): outgoing = turned.reshape(row_count, fsdp_count, col_share)  4.1 us
    all_to_all x1, starting transfers between devices, local(): lax.all_to_all(outgoing, 'fsdp', split_axis=1, concat_axis=0, tiled=True)  3.79 us
    concatenate x1, other arithmetic, local(): ordered_half = jnp.roll(gathered, -owner * owner_rows, axis=0)  3.73 us
    dot_general x1, matrix products, local(): jnp.einsum('cbi,bki->cbk', direction.reshape(col_share, left_blocks, BLOC...  3.12 us
    convert_element_type x1, other arithmetic, local(): second_sum[None].astype(jnp.bfloat16)  3.02 us
  transfers between devices with their start and end apart: 2, of which 1 were waited for; matrix products, arithmetic and copies ran while one was open for 3% of the time, Pallas kernels for 0%

commit v1 on v0

--- a/solution.py
+++ b/solution.py
@@ -12,7 +12,7 @@
 
 
 def clip_of(local_squares, entries):
-    total = lax.psum(local_squares, ("fsdp", "group"))
+    total = lax.psum(lax.psum(local_squares, "group"), "fsdp")
     return jnp.float32(math.sqrt(entries)) / (jnp.sqrt(total) + 1e-06)
 
 

time: 131 us -> 117 us (0.89)
  blocking collectives: 60 us -> 44.4 us
  waiting for transfers between devices: 15.1 us -> 17.1 us
    psum x1 -> x2, blocking collectives: 42.2 us -> 26.6 us  [clip_of(): total = lax.psum(lax.psum(local_squares, 'group'), 'fsdp')]
    all_gather x1, waiting for transfers between devices: 0.02 us -> 2.08 us  [local(): gathered = lax.all_gather(basis_store[0], 'fsdp', axis=0, tiled=True)]
  transfers between devices with their start and end apart: 2 -> 2, of which waited for: 1 -> 2; matrix products, arithmetic and copies ran while one was open for 3% -> 3% of each run, Pallas kernels for 0% -> 0%
where the time goes in v1:
time: 117 us; the launch traced here: 116 us
  blocking collectives  44.4 us (38%)
  local copies, waits for them, and re-layouts  18.6 us (16%)
  waiting for transfers between devices  17.1 us (15%)
  between operations  16.2 us (14%)
  other arithmetic  8.66 us (7%)
  matrix products  7.54 us (6%)
  starting transfers between devices  3.59 us (3%)
    psum x2, blocking collectives, clip_of(): total = lax.psum(lax.psum(local_squares, 'group'), 'fsdp')  26.6 us
    all_to_all x1, blocking collectives, local(): lax.all_to_all(returning, 'fsdp', split_axis=1, concat_axis=0, tiled=True)  17.8 us
    all_to_all x1, waiting for transfers between devices, local(): lax.all_to_all(outgoing, 'fsdp', split_axis=1, concat_axis=0, tiled=True)  14.3 us
    reshape x2, local copies, waits for them, and re-layouts, local(): outgoing = turned.reshape(row_count, fsdp_count, col_share)  4.1 us
    concatenate x1, other arithmetic, local(): ordered_half = jnp.roll(gathered, -owner * owner_rows, axis=0)  3.71 us
    all_to_all x1, starting transfers between devices, local(): lax.all_to_all(outgoing, 'fsdp', split_axis=1, concat_axis=0, tiled=True)  3.56 us
    dot_general x1, matrix products, local(): jnp.einsum('cbi,bki->cbk', direction.reshape(col_share, left_blocks, BLOC...  3.11 us
    convert_element_type x1, other arithmetic, local(): second_sum[None].astype(jnp.bfloat16)  3.02 us
  transfers between devices with their start and end apart: 2, of which 2 were waited for; matrix products, arithmetic and copies ran while one was open for 3% of the time, Pallas kernels for 0%

profile of v1, /device:TPU:0, one launch (start us, length us, event | category | flops | bytes accessed | tf_op | source)
XLA Modules:
  0.0 116.0 jit_solution(82195408698684797)
XLA Ops:
  7.2 0.0 all-gather.3.cloned.1.call-start
  7.2 0.7 all-gather.3.cloned.1.call-update
  7.9 1.9 %multiply_reduce_fusion = f32[]{:T(128)} fusion(bf16[1,64,4096]{2,1,0:T(8,128)(2,1)} %param.6), kind=kLoop, calls=%fused_computation.24 | loop fusion | flops 786431 | bytes 524292 | tf_op jit(solution)/shard_map/reduce_sum | solution.py:30
  9.8 14.1 %psum.14 = f32[]{:T(128)} all-reduce(f32[]{:T(128)} %multiply_reduce_fusion), channel_id=1, replica_groups=mesh['fsdp'=8,'group'=4] {'group'}, use_global_device_ids=true, to_apply=%region_1.2 | all-reduce | flops 1 | bytes 8 | tf_op jit(solution)/shard_map/psum | solution.py:15
  23.9 12.6 %psum.15 = f32[]{:T(128)} all-reduce(f32[]{:T(128)} %psum.14), channel_id=1, replica_groups=mesh['fsdp'=8,'group'=4] {'fsdp'}, use_global_device_ids=true, to_apply=%region_2.3 | all-reduce | flops 1 | bytes 8 | tf_op jit(solution)/shard_map/psum | solution.py:15
  38.5 1.1 copy.42
  39.7 2.1 %all-gather.3.cloned.1.call-done = bf16[1,4608,256]{2,1,0:T(8,128)(2,1)} async-done(((bf16[1,576,256]{2,1,0:T(8,128)(2,1)}), bf16[1,4608,256]{2,1,0:T(8,128)(2,1)}) %all-gather.3.cloned.1.call-update) | async-done | bytes 2359312 | tf_op jit(solution)/shard_map/all_gather | solution.py:31
  41.8 3.7 %fusion = bf16[4608,256]{1,0:T(8,128)(2,1)S(1)} fusion(s32[]{:T(128)S(6)} %select_n.21, bf16[4608,256]{1,0:T(8,128)(2,1)} %bitcast.46), kind=kLoop, calls=%fused_computation.2 | loop fusion | flops 4718592 | bytes 4718596 | tf_op jit(solution)/shard_map/jit(_roll_dynamic)/concatenate | solution.py:34
  45.5 0.0 copy-start
  45.5 0.1 slice.8
  45.6 0.5 fusion.1
  46.1 0.8 copy-done
  46.9 0.6 copy.30
  47.5 1.3 %reshape.80 = f32[64,8,512]{2,1,0:T(8,128)} reshape(f32[64,16,256]{2,1,0:T(8,128)S(1)} %copy.30) | data formatting | bytes 2097152 | tf_op jit(solution)/shard_map/reshape | solution.py:45
  48.8 2.8 %copy.31 = f32[64,8,512]{2,0,1:T(8,128)} copy(f32[64,8,512]{2,1,0:T(8,128)} %reshape.80) | data formatting | bytes 2097152 | tf_op jit(solution)/shard_map/reshape | solution.py:45
  51.6 3.6 %all-to-all-start = ((f32[64,8,512]{2,0,1:T(8,128)}), f32[64,8,512]{2,0,1:T(8,128)S(1)}, u32[]{:S(2)}, u32[]{:S(2)}) async-start(f32[64,8,512]{2,0,1:T(8,128)} %copy.31), calls=%async_computation | async-start | bytes 2097152 | tf_op jit(solution)/shard_map/all_to_all | solution.py:46
  55.2 1.0 slice.9
  56.2 14.3 %all-to-all-done = f32[64,8,512]{2,0,1:T(8,128)S(1)} async-done(((f32[64,8,512]{2,0,1:T(8,128)}), f32[64,8,512]{2,0,1:T(8,128)S(1)}, u32[]{:S(2)}, u32[]{:S(2)}) %all-to-all-start) | async-done | bytes 1048608 | tf_op jit(solution)/shard_map/all_to_all | solution.py:46
  70.5 1.7 %fusion.23 = f32[2,256,512]{2,1,0:T(8,128)} fusion(bf16[2,256,256]{2,1,0:T(8,128)(2,1)S(1)} %bitcast.49, f32[2,256,512]{2,1,0:T(8,128)S(1)} %bitcast.43), kind=kOutput, calls=%fused_computation.32 | convolution fusion | flops 805306368 | bytes 2359296 | tf_op jit(solution)/shard_map/bkc,bki->cbi/dot_general | solution.py:49
  72.2 2.5 %copy.38 = f32[1,512,512]{2,1,0:T(8,128)} copy(f32[1,512,512]{1,2,0:T(8,128)} %bitcast.44) | data formatting | bytes 2097152 | tf_op jit(solution)/shard_map/reshape | solution.py:49
  74.7 3.0 %fusion.14 = (bf16[1,512,512]{2,1,0:T(8,128)(2,1)}, bf16[1,512,512]{2,1,0:T(8,128)(2,1)}, f32[1,512,512]{2,1,0:T(8,128)}, f32[1,512,512]{2,1,0:T(8,128)S(1)}) fusion(f32[1,512,512]{2,1,0:T(8,128)} %copy.38, bf16[1,512,512]{2,1,0:T(8,128)(2,1)} %param.8, bf16[1,512,512]{2,1,0:T(8,128)(2,1)} %param.7), kind=kLoop, calls=%fused_computation.20 | loop fusion | flops 2621440 | bytes 5242880 | tf_op jit(solution)/shard_map/convert_element_type | solution.py:69
  77.8 2.6 %copy.28 = f32[1,512,512]{1,2,0:T(8,128)} copy(f32[1,512,512]{2,1,0:T(8,128)} %get-tuple-element.5) | data formatting | bytes 2097152 | tf_op jit(solution)/shard_map/mul | solution.py:53
  80.4 1.3 %copy.33 = f32[1,512,512]{1,2,0:T(8,128)} copy(f32[1,512,512]{2,1,0:T(8,128)S(1)} %get-tuple-element.6) | data formatting | bytes 2097152 | tf_op jit(solution)/shard_map/mul | solution.py:55
  81.7 3.1 %fusion.4 = f32[2,256,512]{2,1,0:T(8,128)S(1)} fusion(bf16[2,256,256]{2,1,0:T(8,128)(2,1)S(1)} %bitcast.50, f32[512,2,256]{0,2,1:T(8,128)} %bitcast.51, f32[512,2,256]{0,2,1:T(8,128)} %bitcast.52, f32[2,256,512]{2,1,0:T(8,128)} %fusion.23, f32[]{:T(128)} %bitcast.10), kind=kOutput, calls=%fused_computation.12 | convolution fusion | flops 807403520 | bytes 4456452 | tf_op jit(solution)/shard_map/cbi,bki->cbk/dot_general | solution.py:58
  84.8 17.8 %all_to_all.30 = f32[512,8,64]{0,2,1:T(8,128)S(1)} all-to-all(f32[512,8,64]{0,2,1:T(8,128)S(1)} %bitcast.53), channel_id=1, replica_groups=mesh['fsdp'=8,'group'=4] {'fsdp'}, dimensions={1} | all-to-all | bytes 2097152 | tf_op jit(solution)/shard_map/all_to_all | solution.py:62
  102.6 1.6 %copy.35 = f32[8,512,1,64]{1,0,3,2:T(8,128)} copy(f32[8,512,1,64]{1,3,0,2:T(8,128)S(1)} %bitcast.45) | data formatting | bytes 2097152 | tf_op jit(solution)/shard_map/all_to_all | solution.py:62
  104.2 1.4 %reshape_squeeze.11 = f32[16,256,64]{1,0,2:T(8,128)S(1)} reshape(f32[8,512,1,64]{1,0,3,2:T(8,128)} %copy.35) | data formatting | bytes 2097152 | tf_op jit(solution)/shard_map/reshape;squeeze | solution.py:64
  105.6 2.3 %fusion.2 = bf16[64,16,256]{2,0,1:T(8,128)(2,1)S(1)} fusion(bf16[16,256,256]{2,1,0:T(8,128)(2,1)S(1)} %bitcast.42, f32[16,256,64]{1,0,2:T(8,128)S(1)} %reshape_squeeze.11), kind=kOutput, calls=%fused_computation.10 | convolution fusion | flops 805568512 | bytes 3670016 | tf_op jit(solution)/shard_map/blr,bjl->rbj/dot_general | solution.py:65
  107.9 0.3 copy.37
  108.2 1.0 convert_element_type.55
Async XLA Ops:
  7.2 34.6 %all-gather.3.cloned.1.call-start = ((), (), s32[]{:S(2)}) async-start(), calls=%async_computation.2 | async-start | bytes 2654208 | tf_op jit(solution)/shard_map/all_gather | solution.py:31
  45.5 1.4 %copy-start = (bf16[4608,256]{1,0:T(8,128)(2,1)}, bf16[4608,256]{1,0:T(8,128)(2,1)S(1)}, u32[]{:S(2)}) copy-start(bf16[4608,256]{1,0:T(8,128)(2,1)S(1)} %fusion) | copy-start | bytes 7077892
  51.6 18.9 %all-to-all-start = ((f32[64,8,512]{2,0,1:T(8,128)}), f32[64,8,512]{2,0,1:T(8,128)S(1)}, u32[]{:S(2)}, u32[]{:S(2)}) async-start(f32[64,8,512]{2,0,1:T(8,128)} %copy.31), calls=%async_computation | async-start | bytes 2097152 | tf_op jit(solution)/shard_map/all_to_all | solution.py:46
Sparse Core Ops, SparseCore 0:
  9.9 31.8 all-gather.2
